TPU v7x, 512 devices: a whole 4x8x8 slice. The times are simulated.
512 devices in a mesh: dp: 64 (over x, y, core), code: 8 (over z).
Axes of the slice: x: 4, y: 8, z: 8, core: 2. Of those that a mesh axis runs over, the one named last changes fastest.
Arguments:
- items: float32 [65536, 512], P(('dp', 'code')), may hold values from -6 to 6
- codewords: float32 [8192, 512], P('code'), may hold values from -6 to 6
- assign: int32 [65536], P('dp'), may hold values from 0 to 8191, as said below
Outputs:
- new_codewords: float32 [8192, 512], P('code', 'dp')
- residual: float32 [65536, 512], P(('dp', 'code'))
Inputs may be any that keep to these rules, and one draw needn't show every extreme that they name: `assign`: the items are laid out in aligned blocks of 128 (the items of one device). Splitting the codewords into equal ranges, one per index of code, the items of one block name codewords of exactly half of the ranges, 32 items for each such range.
All inputs are finite; a program needn't handle non-finite values.
Results may differ from a plain program's by a relative error of at most 0.0003.
Values sent between devices are 32-bit elements; how exact they have to be, the bound alone decides.
No kernel may reach another device: no remote copies, remote signals or barrier semaphores. Data moves between devices by JAX's collectives and lax.ppermute only.
A program may use at most 64 MiB of HBM per device.

v0:
```python
import jax
import jax.numpy as jnp
from jax import lax
from jax.sharding import PartitionSpec as P

K = 8192
ITERS = 3
epsilon = 1e-05
inverse_temp = 64.0


def unit_rows(values):
    return values * lax.rsqrt(jnp.mean(values * values, axis=-1, keepdims=True) + epsilon)


def kernel_of(rows_block, scaled):
    return jnp.exp(
        jnp.dot(
            unit_rows(rows_block),
            scaled.T,
            precision=lax.Precision.HIGHEST,
            preferred_element_type=jnp.float32,
        )
    )


def column_scale(col_part):
    summed = lax.psum(col_part, "dp")
    return 1.0 / (K * summed)


def row_scaling(row_part, total_items):
    summed = lax.psum(row_part, "code")
    return 1.0 / (total_items * summed)


def body(items, codewords, assign):
    code_count = lax.axis_size("code")
    dp_count = lax.axis_size("dp")
    local_codes = codewords.shape[0]
    width = items.shape[1]
    own_rows = items.shape[0]
    total_items = own_rows * code_count * dp_count
    scaled = unit_rows(codewords) * (inverse_temp / width)
    gathered = lax.all_gather(items, "code", axis=0, tiled=True)
    kernel_vals = kernel_of(gathered, scaled)
    col_part = jnp.sum(kernel_vals, axis=0)
    row_scale = jnp.ones((kernel_vals.shape[0],), jnp.float32)
    for sweep_index in range(ITERS):
        col_scale = column_scale(col_part)
        row_part = jnp.dot(
            kernel_vals,
            col_scale,
            precision=lax.Precision.HIGHEST,
            preferred_element_type=jnp.float32,
        )
        row_scale = row_scaling(row_part, total_items)
        col_part = jnp.dot(
            row_scale,
            kernel_vals,
            precision=lax.Precision.HIGHEST,
            preferred_element_type=jnp.float32,
        )
    mass = lax.psum(col_part, "dp")
    numerator = lax.dot_general(
        kernel_vals,
        row_scale[:, None] * gathered,
        (((0,), (0,)), ((), ())),
        precision=lax.Precision.HIGHEST,
        preferred_element_type=jnp.float32,
    )
    owned_sums = lax.psum_scatter(numerator, "dp", scatter_dimension=1, tiled=True)
    new_codewords = owned_sums / mass[:, None]
    my_code = lax.axis_index("code")
    offset = my_code * local_codes
    index_rows = assign - offset
    inside = (index_rows >= 0) & (index_rows < local_codes)
    picked = jnp.take(codewords, jnp.clip(index_rows, 0, local_codes - 1), axis=0)
    looked = lax.psum_scatter(
        jnp.where(inside[:, None], picked, jnp.float32(0.0)),
        "code",
        scatter_dimension=0,
        tiled=True,
    )
    residual = items - looked
    return (new_codewords, residual)


def solution(mesh):
    in_specs = (P(("dp", "code"), None), P("code", None), P("dp"))
    out_specs = (P("code", "dp"), P(("dp", "code"), None))
    return jax.shard_map(body, mesh=mesh, in_specs=in_specs, out_specs=out_specs, check_vma=False)
```

profile of v0, /device:TPU:16, one launch (start us, length us, event | category | flops | bytes accessed | tf_op | source)
XLA Modules:
  0.0 675.3 jit_solution(14707872022729318664)
XLA Ops:
  7.2 0.0 all-gather.2.cloned.1.call-start
  7.2 0.7 all-gather.2.cloned.1.call-update
  7.9 0.0 reduce-scatter.5.cloned.1.call-start
  7.9 0.7 fusion.23
  8.6 0.0 copy-start.4
  8.6 5.6 gather_fusion
  14.3 0.0 copy-done.4
  14.3 2.0 select_select_fusion
  16.3 0.0 copy-start
  16.3 0.0 reduce-scatter.5.cloned.1.call-update
  16.3 0.0 reduce-scatter.3.cloned.1.call-start
  16.4 1.5 copy-done
  17.9 0.2 multiply_reduce_fusion
  18.1 41.1 %all-gather.2.cloned.1.call-done = f32[1024,512]{1,0:T(8,128)} async-done(((f32[128,512]{1,0:T(8,128)}), f32[1024,512]{1,0:T(8,128)}) %all-gather.2.cloned.1.call-update) | async-done | bytes 2097168 | tf_op jit(solution)/shard_map/all_gather | solution.py:45
  59.2 0.0 copy-start.1
  59.2 2.0 multiply_reduce_fusion.1
  61.2 0.3 copy-done.1
  61.5 9.1 %exponential_reduce_fusion = (f32[1024]{0:T(1024)S(1)}, f32[1024,1024]{1,0:T(8,128)}) fusion(f32[1024,512]{1,0:T(8,128)S(1)} %copy-done, f32[1024]{0:T(1024)S(1)} %add_rsqrt_fusion, f32[1024,512]{1,0:T(8,128)S(1)} %copy-done.1, f32[1024]{0:T(1024)S(1)} %add_rsqrt_fusion.1), kind=kOutput, calls=%fused_computation.15 | convolution fusion | flops 6445071360 | bytes 8400896 | tf_op jit(solution)/shard_map/dot_general | solution.py:18
  70.5 114.3 %psum.49 = f32[1024]{0:T(1024)S(1)} all-reduce(f32[1024]{0:T(1024)S(1)} %get-tuple-element.4), channel_id=1, replica_groups=mesh['dp'=64,'code'=8] {'dp'}, use_global_device_ids=true, to_apply=%region_3.0 | all-reduce | flops 1024 | bytes 8192 | tf_op jit(solution)/shard_map/psum | solution.py:28
  184.8 6.2 fusion.12
  191.0 16.1 %psum.50 = f32[1024]{0:T(1024)S(1)} all-reduce(f32[1024]{0:T(1024)S(1)} %bitcast.21), channel_id=1, replica_groups=mesh['dp'=64,'code'=8] {'code'}, use_global_device_ids=true, to_apply=%region_4.0 | all-reduce | flops 1024 | bytes 8192 | tf_op jit(solution)/shard_map/psum | solution.py:33
  207.1 4.5 fusion.10
  211.6 124.2 %psum.51 = f32[1024]{0:T(1024)S(1)} all-reduce(f32[1024]{0:T(1024)S(1)} %bitcast.23), channel_id=1, replica_groups=mesh['dp'=64,'code'=8] {'dp'}, use_global_device_ids=true, to_apply=%region_5.0 | all-reduce | flops 1024 | bytes 8192 | tf_op jit(solution)/shard_map/psum | solution.py:28
  335.8 6.2 fusion.8
  342.0 14.2 %psum.52 = f32[1024]{0:T(1024)S(1)} all-reduce(f32[1024]{0:T(1024)S(1)} %bitcast.25), channel_id=1, replica_groups=mesh['dp'=64,'code'=8] {'code'}, use_global_device_ids=true, to_apply=%region_6.0 | all-reduce | flops 1024 | bytes 8192 | tf_op jit(solution)/shard_map/psum | solution.py:33
  356.2 4.5 fusion.6
  360.7 124.0 %psum.53 = f32[1024]{0:T(1024)S(1)} all-reduce(f32[1024]{0:T(1024)S(1)} %bitcast.27), channel_id=1, replica_groups=mesh['dp'=64,'code'=8] {'dp'}, use_global_device_ids=true, to_apply=%region_7.0 | all-reduce | flops 1024 | bytes 8192 | tf_op jit(solution)/shard_map/psum | solution.py:28
  484.7 0.0 copy-start.2
  484.7 6.3 fusion.4
  491.1 16.4 %psum.54 = f32[1024]{0:T(1024)S(1)} all-reduce(f32[1024]{0:T(1024)S(1)} %bitcast.29), channel_id=1, replica_groups=mesh['dp'=64,'code'=8] {'code'}, use_global_device_ids=true, to_apply=%region_8.0 | all-reduce | flops 1024 | bytes 8192 | tf_op jit(solution)/shard_map/psum | solution.py:33
  507.4 0.0 copy-done.2
  507.5 10.3 %fusion.2 = f32[1024,512]{0,1:T(8,128)} fusion(f32[1024,1024]{1,0:T(8,128)} %get-tuple-element.5, f32[1024,512]{1,0:T(8,128)S(1)} %copy-done.2, f32[1024]{0:T(1024)S(1)} %multiply_divide_fusion), kind=kOutput, calls=%fused_computation.3 | convolution fusion | flops 6442975232 | bytes 8392704 | tf_op jit(solution)/shard_map/dot_general | solution.py:65
  517.8 0.0 reduce-scatter.3.cloned.1.call-update
  517.8 0.0 copy-start.3
  517.8 4.5 fusion
  522.4 124.2 %psum.55 = f32[1024]{0:T(1024)S(1)} all-reduce(f32[1024]{0:T(1024)S(1)} %bitcast.20), channel_id=1, replica_groups=mesh['dp'=64,'code'=8] {'dp'}, use_global_device_ids=true, to_apply=%region_10.0 | all-reduce | flops 1024 | bytes 8192 | tf_op jit(solution)/shard_map/psum | solution.py:64
  646.6 0.0 reduce-scatter.5.cloned.1.call-done
  646.6 0.0 copy-done.3
  646.6 1.7 sub.11
  648.3 19.1 %reduce-scatter.3.cloned.1.call-done = f32[1024,8]{0,1:T(8,128)} async-done(((f32[1024,512]{0,1:T(8,128)}), f32[1024,8]{0,1:T(8,128)}) %reduce-scatter.3.cloned.1.call-update) | async-done | bytes 32784 | tf_op jit(solution)/shard_map/reduce_scatter | solution.py:72
  667.4 1.4 broadcast_divide_fusion
  (9 shorter events, 0.1 us)
Async XLA Ops:
  7.2 52.1 %all-gather.2.cloned.1.call-start = ((), (), s32[]{:S(2)}) async-start(), calls=%async_computation.2 | async-start | bytes 2359296 | tf_op jit(solution)/shard_map/all_gather | solution.py:45
  7.9 638.7 %reduce-scatter.5.cloned.1.call-start = ((), (), s32[]{:S(2)}) async-start(), calls=%async_computation.4 | async-start | bytes 2359296 | tf_op jit(solution)/shard_map/reduce_scatter | solution.py:79
  8.6 5.6 copy-start.4
  16.3 1.6 copy-start
  16.3 651.1 %reduce-scatter.3.cloned.1.call-start = ((), (), s32[]{:S(2)}) async-start(), calls=%async_computation.3 | async-start | bytes 2129920 | tf_op jit(solution)/shard_map/reduce_scatter | solution.py:72
  59.2 2.2 copy-start.1
  484.7 22.7 %copy-start.2 = (f32[1024,512]{1,0:T(8,128)S(1)}, f32[1024,512]{1,0:T(8,128)}, u32[]{:S(2)}) copy-start(f32[1024,512]{1,0:T(8,128)} %all-gather.2.cloned.1.call-done) | copy-start | bytes 6291460
  517.8 128.8 %copy-start.3 = (f32[128,512]{1,0:T(8,128)S(1)}, f32[128,512]{1,0:T(8,128)}, u32[]{:S(2)}) copy-start(f32[128,512]{1,0:T(8,128)} %param.3) | copy-start | bytes 786436
Sparse Core Ops, SparseCore 0:
  10.1 49.1 all-gather.1
  62.1 43.7 reduce-scatter.4
  517.9 149.3 reduce-scatter.2
where the time goes:
time: 676 us; the launch traced here: 675 us
  blocking collectives  533 us (79%)
  waiting for transfers between devices  60.9 us (9%)
  matrix products  51.6 us (8%)
  between operations  13.9 us (2%)
  other arithmetic  7.99 us (1%)
  local copies, waits for them, and re-layouts  7.4 us (1%)
    psum x3, blocking collectives, column_scale(): summed = lax.psum(col_part, 'dp')  363 us
    psum x1, blocking collectives, body(): mass = lax.psum(col_part, 'dp')  124 us
    psum x3, blocking collectives, row_scaling(): summed = lax.psum(row_part, 'code')  46.7 us
    all_gather x1, waiting for transfers between devices, body(): gathered = lax.all_gather(items, 'code', axis=0, tiled=True)  41.1 us
    reduce_scatter x1, waiting for transfers between devices, body(): lax.psum_scatter(numerator, 'dp', scatter_dimension=1, tiled=True)  19.1 us
    dot_general x3, matrix products, body(): jnp.dot(kernel_vals, col_scale, precision=lax.Precision.HIGHEST, preferre...  18.7 us
  transfers between devices with their start and end apart: 3, of which 2 were waited for; matrix products, arithmetic and copies ran while one was open for 9% of the time, Pallas kernels for 0%

commit v1 on v0

--- a/solution.py
+++ b/solution.py
@@ -61,7 +61,7 @@
             precision=lax.Precision.HIGHEST,
             preferred_element_type=jnp.float32,
         )
-    mass = lax.psum(col_part, "dp")
+    mass = jnp.sum(lax.all_gather(col_part, "dp"), axis=0)
     numerator = lax.dot_general(
         kernel_vals,
         row_scale[:, None] * gathered,

time: 676 us -> 676 us (level)
  waiting for transfers between devices: 60.9 us -> 140 us
  blocking collectives: 533 us -> 454 us
    psum x1 -> x0, blocking collectives: 124 us -> none  [body(): mass = lax.psum(col_part, 'dp')]
    reduce_scatter x1, waiting for transfers between devices: 19.1 us -> 98.5 us  [body(): lax.psum_scatter(numerator, 'dp', scatter_dimension=1, tiled=True)]
    all_gather x0 -> x1, blocking collectives: none -> 44.8 us  [body(): mass = jnp.sum(lax.all_gather(col_part, 'dp'), axis=0)]
where the time goes in v1:
time: 676 us; the launch traced here: 675 us
  blocking collectives  454 us (67%)
  waiting for transfers between devices  140 us (21%)
  matrix products  51.6 us (8%)
  between operations  13.9 us (2%)
  other arithmetic  8.02 us (1%)
  local copies, waits for them, and re-layouts  7.45 us (1%)
    psum x3, blocking collectives, column_scale(): summed = lax.psum(col_part, 'dp')  363 us
    reduce_scatter x1, waiting for transfers between devices, body(): lax.psum_scatter(numerator, 'dp', scatter_dimension=1, tiled=True)  98.5 us
    psum x3, blocking collectives, row_scaling(): summed = lax.psum(row_part, 'code')  46.7 us
    all_gather x1, blocking collectives, body(): mass = jnp.sum(lax.all_gather(col_part, 'dp'), axis=0)  44.8 us
    all_gather x1, waiting for transfers between devices, body(): gathered = lax.all_gather(items, 'code', axis=0, tiled=True)  41.1 us
    dot_general x3, matrix products, body(): jnp.dot(kernel_vals, col_scale, precision=lax.Precision.HIGHEST, preferre...  18.7 us
  transfers between devices with their start and end apart: 3, of which 2 were waited for; matrix products, arithmetic and copies ran while one was open for 9% of the time, Pallas kernels for 0%

profile of v1, /device:TPU:16, one launch (start us, length us, event | category | flops | bytes accessed | tf_op | source)
XLA Modules:
  0.0 675.3 jit_solution(12274452502531287777)
XLA Ops:
  7.2 0.0 all-gather.3.cloned.1.call-start
  7.2 0.7 all-gather.3.cloned.1.call-update
  7.9 0.0 reduce-scatter.5.cloned.1.call-start
  7.9 0.7 fusion.23
  8.6 0.0 copy-start.4
  8.6 5.6 gather_fusion
  14.3 0.0 copy-done.4
  14.3 2.0 select_select_fusion
  16.3 0.0 copy-start
  16.3 0.0 reduce-scatter.5.cloned.1.call-update
  16.3 0.0 reduce-scatter.3.cloned.1.call-start
  16.4 1.5 copy-done
  17.9 0.2 multiply_reduce_fusion
  18.1 41.1 %all-gather.3.cloned.1.call-done = f32[1024,512]{1,0:T(8,128)} async-done(((f32[128,512]{1,0:T(8,128)}), f32[1024,512]{1,0:T(8,128)}) %all-gather.3.cloned.1.call-update) | async-done | bytes 2097168 | tf_op jit(solution)/shard_map/all_gather | solution.py:45
  59.2 0.0 copy-start.1
  59.2 2.0 multiply_reduce_fusion.1
  61.2 0.3 copy-done.1
  61.5 9.1 %exponential_reduce_fusion = (f32[1024]{0:T(1024)S(1)}, f32[1024,1024]{1,0:T(8,128)}) fusion(f32[1024,512]{1,0:T(8,128)S(1)} %copy-done, f32[1024]{0:T(1024)S(1)} %add_rsqrt_fusion, f32[1024,512]{1,0:T(8,128)S(1)} %copy-done.1, f32[1024]{0:T(1024)S(1)} %add_rsqrt_fusion.1), kind=kOutput, calls=%fused_computation.15 | convolution fusion | flops 6445071360 | bytes 8400896 | tf_op jit(solution)/shard_map/dot_general | solution.py:18
  70.5 114.3 %psum.42 = f32[1024]{0:T(1024)S(1)} all-reduce(f32[1024]{0:T(1024)S(1)} %get-tuple-element.4), channel_id=1, replica_groups=mesh['dp'=64,'code'=8] {'dp'}, use_global_device_ids=true, to_apply=%region_3.0 | all-reduce | flops 1024 | bytes 8192 | tf_op jit(solution)/shard_map/psum | solution.py:28
  184.8 6.2 fusion.12
  191.0 16.1 %psum.43 = f32[1024]{0:T(1024)S(1)} all-reduce(f32[1024]{0:T(1024)S(1)} %bitcast.21), channel_id=1, replica_groups=mesh['dp'=64,'code'=8] {'code'}, use_global_device_ids=true, to_apply=%region_4.0 | all-reduce | flops 1024 | bytes 8192 | tf_op jit(solution)/shard_map/psum | solution.py:33
  207.1 4.5 fusion.10
  211.6 124.2 %psum.44 = f32[1024]{0:T(1024)S(1)} all-reduce(f32[1024]{0:T(1024)S(1)} %bitcast.23), channel_id=1, replica_groups=mesh['dp'=64,'code'=8] {'dp'}, use_global_device_ids=true, to_apply=%region_5.0 | all-reduce | flops 1024 | bytes 8192 | tf_op jit(solution)/shard_map/psum | solution.py:28
  335.8 6.2 fusion.8
  342.0 14.2 %psum.45 = f32[1024]{0:T(1024)S(1)} all-reduce(f32[1024]{0:T(1024)S(1)} %bitcast.25), channel_id=1, replica_groups=mesh['dp'=64,'code'=8] {'code'}, use_global_device_ids=true, to_apply=%region_6.0 | all-reduce | flops 1024 | bytes 8192 | tf_op jit(solution)/shard_map/psum | solution.py:33
  356.2 4.5 fusion.6
  360.7 124.0 %psum.46 = f32[1024]{0:T(1024)S(1)} all-reduce(f32[1024]{0:T(1024)S(1)} %bitcast.27), channel_id=1, replica_groups=mesh['dp'=64,'code'=8] {'dp'}, use_global_device_ids=true, to_apply=%region_7.0 | all-reduce | flops 1024 | bytes 8192 | tf_op jit(solution)/shard_map/psum | solution.py:28
  484.7 0.0 copy-start.2
  484.7 6.3 fusion.4
  491.1 16.4 %psum.47 = f32[1024]{0:T(1024)S(1)} all-reduce(f32[1024]{0:T(1024)S(1)} %bitcast.29), channel_id=1, replica_groups=mesh['dp'=64,'code'=8] {'code'}, use_global_device_ids=true, to_apply=%region_8.0 | all-reduce | flops 1024 | bytes 8192 | tf_op jit(solution)/shard_map/psum | solution.py:33
  507.4 0.0 copy-done.2
  507.5 10.3 %fusion.2 = f32[1024,512]{0,1:T(8,128)} fusion(f32[1024,1024]{1,0:T(8,128)} %get-tuple-element.5, f32[1024,512]{1,0:T(8,128)S(1)} %copy-done.2, f32[1024]{0:T(1024)S(1)} %multiply_divide_fusion), kind=kOutput, calls=%fused_computation.3 | convolution fusion | flops 6442975232 | bytes 8392704 | tf_op jit(solution)/shard_map/dot_general | solution.py:65
  517.8 0.0 reduce-scatter.3.cloned.1.call-update
  517.8 0.0 copy-start.3
  517.8 4.5 fusion
  522.4 44.8 %all-gather = f32[65536]{0:T(1024)S(1)} all-gather(f32[1024]{0:T(1024)S(1)} %bitcast.19), channel_id=2, replica_groups=mesh['dp'=64,'code'=8] {'dp'}, dimensions={0}, use_global_device_ids=true | all-gather | bytes 266240 | tf_op jit(solution)/shard_map/all_gather | solution.py:64
  567.2 0.0 reduce-scatter.5.cloned.1.call-done
  567.2 0.0 copy-done.3
  567.2 1.7 sub.11
  568.9 98.5 %reduce-scatter.3.cloned.1.call-done = f32[1024,8]{0,1:T(8,128)} async-done(((f32[1024,512]{0,1:T(8,128)}), f32[1024,8]{0,1:T(8,128)}) %reduce-scatter.3.cloned.1.call-update) | async-done | bytes 32784 | tf_op jit(solution)/shard_map/reduce_scatter | solution.py:72
  667.4 1.4 broadcast_divide_fusion
  (11 shorter events, 0.1 us)
Async XLA Ops:
  7.2 52.1 %all-gather.3.cloned.1.call-start = ((), (), s32[]{:S(2)}) async-start(), calls=%async_computation.2 | async-start | bytes 2359296 | tf_op jit(solution)/shard_map/all_gather | solution.py:45
  7.9 559.3 %reduce-scatter.5.cloned.1.call-start = ((), (), s32[]{:S(2)}) async-start(), calls=%async_computation.4 | async-start | bytes 2359296 | tf_op jit(solution)/shard_map/reduce_scatter | solution.py:79
  8.6 5.6 copy-start.4
  16.3 1.6 copy-start
  16.3 651.1 %reduce-scatter.3.cloned.1.call-start = ((), (), s32[]{:S(2)}) async-start(), calls=%async_computation.3 | async-start | bytes 2129920 | tf_op jit(solution)/shard_map/reduce_scatter | solution.py:72
  59.2 2.2 copy-start.1
  484.7 22.7 %copy-start.2 = (f32[1024,512]{1,0:T(8,128)S(1)}, f32[1024,512]{1,0:T(8,128)}, u32[]{:S(2)}) copy-start(f32[1024,512]{1,0:T(8,128)} %all-gather.3.cloned.1.call-done) | copy-start | bytes 6291460
  517.8 49.4 %copy-start.3 = (f32[128,512]{1,0:T(8,128)S(1)}, f32[128,512]{1,0:T(8,128)}, u32[]{:S(2)}) copy-start(f32[128,512]{1,0:T(8,128)} %param.3) | copy-start | bytes 786436
Sparse Core Ops, SparseCore 0:
  10.1 49.1 all-gather.2
  62.1 43.7 reduce-scatter.4
  517.9 149.4 reduce-scatter.2

commit v2 on v0

--- a/solution.py
+++ b/solution.py
@@ -42,7 +42,9 @@
     own_rows = items.shape[0]
     total_items = own_rows * code_count * dp_count
     scaled = unit_rows(codewords) * (inverse_temp / width)
-    gathered = lax.all_gather(items, "code", axis=0, tiled=True)
+    gathered = jnp.concatenate(
+        lax.all_to_all(jnp.stack([items] * lax.axis_size("code")), "code", 0, 0), axis=0
+    )
     kernel_vals = kernel_of(gathered, scaled)
     col_part = jnp.sum(kernel_vals, axis=0)
     row_scale = jnp.ones((kernel_vals.shape[0],), jnp.float32)

time: 676 us -> 703 us (1.040)
  waiting for transfers between devices: 60.9 us -> 71.4 us
  starting transfers between devices: 0.12 us -> 10.5 us
    all_to_all x0 -> x1, waiting for transfers between devices: none -> 52.1 us  [body(): lax.all_to_all(jnp.stack([items] * lax.axis_size('code')), 'code', 0, 0)]
    all_gather x1 -> x0, waiting for transfers between devices: 41.1 us -> none  [body(): gathered = lax.all_gather(items, 'code', axis=0, tiled=True)]
    all_to_all x0 -> x1, starting transfers between devices: none -> 10.4 us  [body(): lax.all_to_all(jnp.stack([items] * lax.axis_size('code')), 'code', 0, 0)]
where the time goes in v2:
time: 703 us; the launch traced here: 702 us
  blocking collectives  536 us (76%)
  waiting for transfers between devices  71.4 us (10%)
  matrix products  49.5 us (7%)
  between operations  14.2 us (2%)
  other arithmetic  12.1 us (2%)
  starting transfers between devices  10.5 us (1%)
  local copies, waits for them, and re-layouts  8.35 us (1%)
    psum x3, blocking collectives, column_scale(): summed = lax.psum(col_part, 'dp')  367 us
    psum x1, blocking collectives, body(): mass = lax.psum(col_part, 'dp')  124 us
    all_to_all x1, waiting for transfers between devices, body(): lax.all_to_all(jnp.stack([items] * lax.axis_size('code')), 'code', 0, 0)  52.1 us
    psum x3, blocking collectives, row_scaling(): summed = lax.psum(row_part, 'code')  44.7 us
    reduce_scatter x1, waiting for transfers between devices, body(): lax.psum_scatter(numerator, 'dp', scatter_dimension=1, tiled=True)  19.3 us
    dot_general x3, matrix products, body(): jnp.dot(kernel_vals, col_scale, precision=lax.Precision.HIGHEST, preferre...  18.5 us
  transfers between devices with their start and end apart: 3, of which 2 were waited for; matrix products, arithmetic and copies ran while one was open for 9% of the time, Pallas kernels for 0%

profile of v2, /device:TPU:16, one launch (start us, length us, event | category | flops | bytes accessed | tf_op | source)
XLA Modules:
  0.0 702.0 jit_solution(9531580389538227329)
XLA Ops:
  7.2 2.6 stack.2
  9.7 0.0 copy-start.3
  9.7 0.0 copy-start.1
  9.7 10.4 %all-to-all-start = ((f32[8,128,512]{2,1,0:T(8,128)}), f32[8,128,512]{2,1,0:T(8,128)}, u32[]{:S(2)}, u32[]{:S(2)}) async-start(f32[8,128,512]{2,1,0:T(8,128)} %stack.2), calls=%async_computation | async-start | bytes 4194304 | tf_op jit(solution)/shard_map/all_to_all | solution.py:46
  20.2 0.0 reduce-scatter.5.cloned.1.call-start
  20.2 0.0 copy-done.3
  20.3 0.0 copy-done.1
  20.3 4.9 gather_fusion
  25.2 3.1 select_select_fusion
  28.3 0.0 reduce-scatter.5.cloned.1.call-update
  28.4 0.0 reduce-scatter.3.cloned.1.call-start
  28.4 0.2 multiply_reduce_fusion
  28.6 52.1 %all-to-all-done = f32[8,128,512]{2,1,0:T(8,128)} async-done(((f32[8,128,512]{2,1,0:T(8,128)}), f32[8,128,512]{2,1,0:T(8,128)}, u32[]{:S(2)}, u32[]{:S(2)}) %all-to-all-start) | async-done | bytes 2097184 | tf_op jit(solution)/shard_map/all_to_all | solution.py:46
  80.7 1.8 multiply_reduce_fusion.1
  82.6 1.8 bitcast_multiply_fusion.1
  84.4 9.1 %exponential_reduce_fusion = (f32[1024]{0:T(1024)S(1)}, f32[1024,1024]{1,0:T(8,128)}) fusion(f32[1024,512]{1,0:T(8,128)S(1)} %bitcast_multiply_fusion.1, f32[1024,512]{1,0:T(8,128)S(1)} %copy-done.1, f32[1024]{0:T(1024)S(1)} %add_rsqrt_fusion), kind=kOutput, calls=%fused_computation.15 | convolution fusion | flops 6444547072 | bytes 8396800 | tf_op jit(solution)/shard_map/dot_general | solution.py:18
  93.5 119.0 %psum.49 = f32[1024]{0:T(1024)S(1)} all-reduce(f32[1024]{0:T(1024)S(1)} %get-tuple-element.4), channel_id=1, replica_groups=mesh['dp'=64,'code'=8] {'dp'}, use_global_device_ids=true, to_apply=%region_3.0 | all-reduce | flops 1024 | bytes 8192 | tf_op jit(solution)/shard_map/psum | solution.py:28
  212.4 6.2 fusion.12
  218.6 14.2 %psum.50 = f32[1024]{0:T(1024)S(1)} all-reduce(f32[1024]{0:T(1024)S(1)} %bitcast.28), channel_id=1, replica_groups=mesh['dp'=64,'code'=8] {'code'}, use_global_device_ids=true, to_apply=%region_4.0 | all-reduce | flops 1024 | bytes 8192 | tf_op jit(solution)/shard_map/psum | solution.py:33
  232.7 4.5 fusion.10
  237.2 124.2 %psum.51 = f32[1024]{0:T(1024)S(1)} all-reduce(f32[1024]{0:T(1024)S(1)} %bitcast.30), channel_id=1, replica_groups=mesh['dp'=64,'code'=8] {'dp'}, use_global_device_ids=true, to_apply=%region_5.0 | all-reduce | flops 1024 | bytes 8192 | tf_op jit(solution)/shard_map/psum | solution.py:28
  361.5 6.2 fusion.8
  367.6 16.2 %psum.52 = f32[1024]{0:T(1024)S(1)} all-reduce(f32[1024]{0:T(1024)S(1)} %bitcast.32), channel_id=1, replica_groups=mesh['dp'=64,'code'=8] {'code'}, use_global_device_ids=true, to_apply=%region_6.0 | all-reduce | flops 1024 | bytes 8192 | tf_op jit(solution)/shard_map/psum | solution.py:33
  383.8 4.5 fusion.6
  388.3 124.0 %psum.53 = f32[1024]{0:T(1024)S(1)} all-reduce(f32[1024]{0:T(1024)S(1)} %bitcast.34), channel_id=1, replica_groups=mesh['dp'=64,'code'=8] {'dp'}, use_global_device_ids=true, to_apply=%region_7.0 | all-reduce | flops 1024 | bytes 8192 | tf_op jit(solution)/shard_map/psum | solution.py:28
  512.3 6.2 fusion.4
  518.5 14.4 %psum.54 = f32[1024]{0:T(1024)S(1)} all-reduce(f32[1024]{0:T(1024)S(1)} %bitcast.36), channel_id=1, replica_groups=mesh['dp'=64,'code'=8] {'code'}, use_global_device_ids=true, to_apply=%region_8.0 | all-reduce | flops 1024 | bytes 8192 | tf_op jit(solution)/shard_map/psum | solution.py:33
  532.9 0.0 copy-start
  532.9 1.9 bitcast_multiply_fusion
  534.8 0.9 copy-done
  535.7 8.4 %fusion.2 = f32[1024,512]{0,1:T(8,128)} fusion(f32[1024,512]{1,0:T(8,128)S(1)} %bitcast_multiply_fusion, f32[1024,1024]{1,0:T(8,128)S(1)} %copy-done), kind=kOutput, calls=%fused_computation.3 | convolution fusion | flops 6442450944 | bytes 8388608 | tf_op jit(solution)/shard_map/dot_general | solution.py:67
  544.1 0.0 reduce-scatter.3.cloned.1.call-update
  544.2 0.0 copy-start.2
  544.2 4.5 fusion
  548.7 124.1 %psum.55 = f32[1024]{0:T(1024)S(1)} all-reduce(f32[1024]{0:T(1024)S(1)} %bitcast.27), channel_id=1, replica_groups=mesh['dp'=64,'code'=8] {'dp'}, use_global_device_ids=true, to_apply=%region_10.0 | all-reduce | flops 1024 | bytes 8192 | tf_op jit(solution)/shard_map/psum | solution.py:66
  672.8 0.0 reduce-scatter.5.cloned.1.call-done
  672.8 0.0 copy-done.2
  672.8 1.7 sub.11
  674.5 19.3 %reduce-scatter.3.cloned.1.call-done = f32[1024,8]{0,1:T(8,128)} async-done(((f32[1024,512]{0,1:T(8,128)}), f32[1024,8]{0,1:T(8,128)}) %reduce-scatter.3.cloned.1.call-update) | async-done | bytes 32784 | tf_op jit(solution)/shard_map/reduce_scatter | solution.py:74
  693.8 1.4 broadcast_divide_fusion
  (10 shorter events, 0.1 us)
Async XLA Ops:
  9.7 10.5 %copy-start.3 = (s32[1024]{0:T(1024)S(1)}, s32[1024]{0:T(1024)}, u32[]{:S(2)}) copy-start(s32[1024]{0:T(1024)} %param.5) | copy-start | bytes 12292
  9.7 10.5 %copy-start.1 = (f32[1024,512]{1,0:T(8,128)S(1)}, f32[1024,512]{1,0:T(8,128)}, u32[]{:S(2)}) copy-start(f32[1024,512]{1,0:T(8,128)} %param.4) | copy-start | bytes 6291460
  9.7 71.0 %all-to-all-start = ((f32[8,128,512]{2,1,0:T(8,128)}), f32[8,128,512]{2,1,0:T(8,128)}, u32[]{:S(2)}, u32[]{:S(2)}) async-start(f32[8,128,512]{2,1,0:T(8,128)} %stack.2), calls=%async_computation | async-start | bytes 4194304 | tf_op jit(solution)/shard_map/all_to_all | solution.py:46
  20.2 652.6 %reduce-scatter.5.cloned.1.call-start = ((), (), s32[]{:S(2)}) async-start(), calls=%async_computation.4 | async-start | bytes 2359296 | tf_op jit(solution)/shard_map/reduce_scatter | solution.py:81
  28.4 665.4 %reduce-scatter.3.cloned.1.call-start = ((), (), s32[]{:S(2)}) async-start(), calls=%async_computation.3 | async-start | bytes 2129920 | tf_op jit(solution)/shard_map/reduce_scatter | solution.py:74
  532.9 2.8 copy-start
  544.2 128.6 %copy-start.2 = (f32[128,512]{1,0:T(8,128)S(1)}, f32[128,512]{1,0:T(8,128)}, u32[]{:S(2)}) copy-start(f32[128,512]{1,0:T(8,128)} %param.3) | copy-start | bytes 786436
Sparse Core Ops, SparseCore 0:
  28.5 63.7 reduce-scatter.4
  544.3 149.4 reduce-scatter.2
